TPU v7x, 32 devices: a whole 2x2x4 slice. The times are simulated.
32 devices in a mesh: seq: 4 (over y, x), res: 8 (over z, core).
Axes of the slice: x: 2, y: 2, z: 4, core: 2. Of those that a mesh axis runs over, the one named last changes fastest.
Arguments:
- alignment: float32 [256, 64, 256], P('seq', 'res'), may hold values from -100 to 100
- pair_features: float32 [64, 64, 128], P('seq', 'res'), may hold values from -100 to 100
- outer_gain: float32 [256], replicated, may hold values from 0.5 to 1.5
- w_outer_in: float32 [256, 64], replicated, may hold values from -0.375 to 0.375
- w_outer_out: float32 [1024, 128], replicated, may hold values from -0.1875 to 0.1875
- pair_gain: float32 [128], replicated, may hold values from 0.5 to 1.5
- w_bias: float32 [128, 8], replicated, may hold values from -30 to 30
- row_gain: float32 [256], replicated, may hold values from 0.5 to 1.5
- w_project: float32 [256, 1024], replicated, may hold values from -0.375 to 0.375
- w_output: float32 [256, 256], replicated, may hold values from -0.375 to 0.375
Outputs:
- alignment_out: float32 [256, 64, 256], P('seq', 'res')
- updated_pair_array: float32 [64, 64, 128], P('seq', 'res')
All inputs are finite; a program needn't handle non-finite values.
Results may differ from a plain program's by a relative error of at most 0.00018.
Values sent between devices are 32-bit elements; how exact they have to be, the bound alone decides.
A program may use at most 128 MiB of HBM per device.

v0:
```python
import jax
import jax.numpy as jnp
from jax import lax
from jax.sharding import PartitionSpec as P

precise = lax.Precision.HIGHEST


def layer_norm(values, scales):
    average = jnp.mean(values, axis=-1, keepdims=True)
    centered = values - average
    variance = jnp.mean(centered * centered, axis=-1, keepdims=True)
    return centered * lax.rsqrt(variance + 1e-05) * scales


def row_attention(sequence, bias_all, row_gain, w_project, w_output):
    residues, channels = sequence.shape
    head_count = bias_all.shape[0]
    head_size = channels // head_count
    normed_rows = layer_norm(sequence, row_gain)
    projected = jnp.dot(
        normed_rows, w_project, precision=precise, preferred_element_type=jnp.float32
    )
    query_map = projected[:, :channels].reshape(residues, head_count, head_size) * head_size ** (
        -0.5
    )
    key_map = projected[:, channels : 2 * channels].reshape(residues, head_count, head_size)
    value_map = projected[:, 2 * channels : 3 * channels].reshape(residues, head_count, head_size)
    gate_map = projected[:, 3 * channels :]
    scores = jnp.einsum("ihd,jhd->hij", query_map, key_map, precision=precise) + bias_all
    weights = jax.nn.softmax(scores, axis=-1)
    mixed_heads = jnp.einsum("hij,jhd->ihd", weights, value_map, precision=precise).reshape(
        residues, channels
    )
    gated_out = jax.nn.sigmoid(gate_map) * mixed_heads
    return sequence + jnp.dot(
        gated_out, w_output, precision=precise, preferred_element_type=jnp.float32
    )


def on_device(
    alignment,
    pair_features,
    outer_gain,
    w_outer_in,
    w_outer_out,
    pair_gain,
    w_bias,
    row_gain,
    w_project,
    w_output,
):
    sequence_local_count, residue_local_count, alignment_channel_count = alignment.shape
    row_block = pair_features.shape[0]
    sequence_group_list = lax.axis_size("res")
    seq_groups = lax.axis_size("seq")
    seq_total = sequence_local_count * seq_groups
    channels = w_outer_in.shape[1] // 2
    normed_rows = layer_norm(alignment, outer_gain)
    both_maps = jnp.einsum("src,cd->sdr", normed_rows, w_outer_in, precision=precise)
    left_maps = both_maps[:, :channels]
    right_maps = both_maps[:, channels:]
    left_all = lax.all_gather(left_maps, "res", axis=2, tiled=True)
    left_rows = lax.all_to_all(left_all, "seq", split_axis=2, concat_axis=0, tiled=True)
    product = jnp.einsum(
        "sxi,syj->ijxy",
        left_rows,
        lax.all_gather(right_maps, "seq", axis=0, tiled=True),
        precision=precise,
    )
    summed = product.reshape(row_block, residue_local_count, channels * channels)
    pair_update = jnp.einsum("ijk,kc->ijc", summed / seq_total, w_outer_out, precision=precise)
    updated_pair_array = pair_features + pair_update
    bias_tile = jnp.einsum(
        "ijc,ch->hij", layer_norm(updated_pair_array, pair_gain), w_bias, precision=precise
    )
    bias_rows = lax.all_gather(bias_tile, "res", axis=2, tiled=True)
    bias_all = lax.all_gather(bias_rows, "seq", axis=1, tiled=True)
    sequence_grouped_rows = alignment.reshape(
        sequence_group_list,
        sequence_local_count // sequence_group_list,
        residue_local_count,
        alignment_channel_count,
    )
    sequences = lax.all_to_all(
        sequence_grouped_rows, "res", split_axis=0, concat_axis=2, tiled=True
    )[0]
    updated = jax.vmap(row_attention, in_axes=(0, None, None, None, None))(
        sequences, bias_all, row_gain, w_project, w_output
    )
    attended = updated[None]
    returned_result = lax.all_to_all(attended, "res", split_axis=2, concat_axis=0, tiled=True)
    return (
        returned_result.reshape(sequence_local_count, residue_local_count, alignment_channel_count),
        updated_pair_array,
    )


def solution(mesh):
    in_specs = (
        P("seq", "res", None),
        P("seq", "res", None),
        P(),
        P(),
        P(),
        P(),
        P(),
        P(),
        P(),
        P(),
    )
    out_specs = (P("seq", "res", None), P("seq", "res", None))
    return jax.shard_map(
        on_device, mesh=mesh, in_specs=in_specs, out_specs=out_specs, check_vma=False
    )
```

profile of v0, /device:TPU:0, one launch (start us, length us, event | category | flops | bytes accessed | tf_op | source)
XLA Modules:
  0.0 148.9 jit_solution(3641051938862273192)
XLA Ops:
  0.6 0.0 copy-start
  0.6 1.3 reduce_sum.65
  1.9 1.3 multiply_reduce_fusion
  3.2 1.7 %convolution_bitcast_fusion = f32[64,64,8]{1,2,0:T(8,128)S(1)} fusion(f32[64,8,256]{2,1,0:T(8,128)} %param.10, f32[256]{0:T(256)} %param.12, f32[64,8]{1,0:T(8,128)S(1)} %add_rsqrt_fusion, f32[64,8]{1,0:T(8,128)S(1)} %broadcast_multiply_fusion, f32[256,64]{0,1:T(8,128)} %param.13), kind=kOutput, calls=%fused_computation.8 | convolution fusion | flops 101056512 | bytes 726016 | tf_op jit(solution)/shard_map/src,cd->sdr/dot_general | solution.py:60
  4.9 0.1 fusion.40
  5.1 25.1 %all_gather.13 = f32[64,32,64]{1,2,0:T(8,128)S(1)} all-gather(f32[64,32,8]{1,2,0:T(8,128)S(1)} %get-tuple-element.5), channel_id=1, replica_groups=mesh['seq'=4,'res'=8] {'res'}, dimensions={2}, use_global_device_ids=true | all-gather | bytes 589824 | tf_op jit(solution)/shard_map/all_gather | solution.py:63
  30.2 2.1 %copy.39 = f32[64,32,64]{0,1,2:T(8,128)} copy(f32[64,32,64]{1,2,0:T(8,128)S(1)} %all_gather.13) | data formatting | bytes 1048576 | tf_op jit(solution)/shard_map/all_gather | solution.py:63
  32.3 2.7 %reshape.99 = f32[4,1,32768]{2,1,0:T(1,128)} reshape(f32[64,32,64]{2,1,0:T(8,128)} %bitcast.73) | data formatting | bytes 1048576
  35.0 3.7 %all-to-all-start.1 = ((f32[4,1,32768]{2,1,0:T(1,128)}), f32[4,1,32768]{2,1,0:T(1,128)S(1)}, u32[]{:S(2)}, u32[]{:S(2)}) async-start(f32[4,1,32768]{2,1,0:T(1,128)} %reshape.99), calls=%async_computation.1 | async-start | bytes 1048576 | tf_op jit(solution)/shard_map/all_to_all | solution.py:64
  38.7 18.5 %all_gather.12 = f32[256,32,8]{1,2,0:T(8,128)S(1)} all-gather(f32[64,32,8]{1,2,0:T(8,128)S(1)} %get-tuple-element.6), channel_id=1, replica_groups=mesh['seq'=4,'res'=8] {'seq'}, dimensions={0}, use_global_device_ids=true | all-gather | bytes 327680 | tf_op jit(solution)/shard_map/all_gather | solution.py:68
  57.2 0.4 copy.49
  57.6 4.3 %all-to-all-start = ((f32[8,8,8,256]{3,2,1,0:T(8,128)}), f32[8,8,8,256]{3,2,1,0:T(8,128)}, u32[]{:S(2)}, u32[]{:S(2)}) async-start(f32[8,8,8,256]{3,2,1,0:T(8,128)} %bitcast), calls=%async_computation | async-start | bytes 1048576 | tf_op jit(solution)/shard_map/all_to_all | solution.py:85
  62.0 0.5 broadcast.97
  62.5 2.1 %reduce.2 = f32[4,32768]{1,0:T(4,128)S(1)} reduce(f32[4,1,32768]{2,1,0:T(1,128)S(1)} %all-to-all-done.1, f32[]{:T(128)} %broadcast.97), dimensions={1}, to_apply=%all_to_all.38.reduce_sub_computation | reduce | bytes 1048580 | tf_op jit(solution)/shard_map/all_to_all | solution.py:64
  64.6 0.5 reshape.100
  65.2 0.7 copy.59
  65.9 0.6 reshape.94
  66.5 3.2 %multiply_bitcast_fusion = f32[16,8,32,32]{2,1,0,3:T(8,128)} fusion(f32[256,32,8,1]{0,2,3,1:T(8,128)S(1)} %copy.49, f32[256,32,16,1]{0,1,2,3:T(8,128)S(1)} %reshape.94), kind=kOutput, calls=%fused_computation.3 | convolution fusion | flops 402784256 | bytes 1310720 | tf_op jit(solution)/shard_map/sxi,syj->ijxy/dot_general | solution.py:65
  69.7 2.3 %copy.42 = f32[16,8,32,32]{3,2,1,0:T(8,128)S(1)} copy(f32[16,8,32,32]{2,1,0,3:T(8,128)} %multiply_bitcast_fusion) | data formatting | bytes 1048576 | tf_op jit(solution)/shard_map/div | solution.py:72
  71.9 0.0 copy-start.6
  72.0 1.7 %div.50 = f32[16,8,1024]{2,1,0:T(8,128)} reshape(f32[16,8,32,32]{3,2,1,0:T(8,128)S(1)} %copy.42) | data formatting | bytes 1048576 | tf_op jit(solution)/shard_map/div | solution.py:72
  73.7 1.9 %fusion.41 = (f32[16,8]{1,0:T(8,128)S(1)}, f32[16,8,128]{2,1,0:T(8,128)S(1)}) fusion(f32[16,8,128]{2,1,0:T(8,128)S(1)} %copy-done.3, f32[16,8,1024]{2,1,0:T(8,128)} %div.50, f32[1024,128]{1,0:T(8,128)} %param.14), kind=kOutput, calls=%fused_computation.60 | convolution fusion | flops 201359232 | bytes 1180160 | tf_op jit(solution)/shard_map/ijk,kc->ijc/dot_general | solution.py:72
  75.6 0.0 copy-start.2
  75.6 0.0 copy-start.4
  75.7 0.2 multiply_reduce_fusion.2
  75.8 0.3 convolution_bitcast_fusion.1
  76.1 14.9 %all_gather.14 = f32[8,16,64]{0,2,1:T(8,128)S(1)} all-gather(f32[8,16,8]{0,2,1:T(8,128)S(1)} %convolution_bitcast_fusion.1), channel_id=1, replica_groups=mesh['seq'=4,'res'=8] {'res'}, dimensions={2}, use_global_device_ids=true | all-gather | bytes 36864 | tf_op jit(solution)/shard_map/all_gather | solution.py:77
  91.1 0.2 copy.43
  91.2 8.4 %all_gather.15 = f32[8,64,64]{2,0,1:T(8,128)S(1)} all-gather(f32[8,16,64]{2,0,1:T(8,128)S(1)} %copy.43), channel_id=1, replica_groups=mesh['seq'=4,'res'=8] {'seq'}, dimensions={1}, use_global_device_ids=true | all-gather | bytes 163840 | tf_op jit(solution)/shard_map/all_gather | solution.py:78
  99.6 0.1 copy.44
  99.8 1.2 bitcast_reduce_fusion
  101.0 0.1 div.42
  101.1 1.3 multiply_reduce_fusion.1
  102.4 0.1 rsqrt.28
  102.5 2.9 %fusion.4 = f32[8,64,1024]{2,1,0:T(8,128)S(1)} fusion(f32[256,1024]{1,0:T(8,128)S(1)} %copy-done, f32[256]{0:T(256)S(1)} %copy-done.4, f32[8,64]{1,0:T(8,128)S(1)} %rsqrt.28, f32[8,64]{1,0:T(8,128)S(1)} %div.42, f32[8,8,8,256]{3,2,1,0:T(8,128)} %all-to-all-done), kind=kOutput, calls=%fused_computation.11 | convolution fusion | flops 1611005952 | bytes 3675136 | tf_op jit(solution)/shard_map/vmap()/dot_general | solution.py:21
  105.5 1.2 fusion.39
  106.7 2.4 %copy.38 = f32[8,64,256]{1,2,0:T(8,128)} copy(f32[8,64,256]{2,1,0:T(8,128)} %get-tuple-element.2) | data formatting | bytes 1048576 | tf_op jit(solution)/shard_map/vmap()/slice | solution.py:27
  109.1 2.4 %copy.37 = f32[8,64,256]{1,2,0:T(8,128)} copy(f32[8,64,256]{2,1,0:T(8,128)} %get-tuple-element.3) | data formatting | bytes 1048576 | tf_op jit(solution)/shard_map/vmap()/mul | solution.py:24
  111.5 2.4 %copy.36 = f32[8,64,256]{1,2,0:T(8,128)} copy(f32[8,64,256]{2,1,0:T(8,128)} %get-tuple-element.4) | data formatting | bytes 1048576 | tf_op jit(solution)/shard_map/vmap()/slice | solution.py:28
  113.8 5.1 %add_reduce_fusion = (f32[8,8,64]{2,1,0:T(8,128)S(1)}, f32[8,8,64,64]{2,3,1,0:T(8,128)S(1)}) fusion(f32[8,64,64]{1,2,0:T(8,128)S(1)} %copy.44, f32[8,64,8,32]{1,3,2,0:T(8,128)} %bitcast.72, f32[8,64,8,32]{1,3,2,0:T(8,128)} %bitcast.71), kind=kOutput, calls=%fused_computation.4 | convolution fusion | flops 101183488 | bytes 2244608 | tf_op jit(solution)/shard_map/vmap(ihd,jhd->hij)/dot_general | solution.py:30
  119.0 0.5 fusion.2
  119.5 0.7 copy-done.1
  120.2 3.3 %fusion = f32[8,8,32,64]{3,2,1,0:T(8,128)} fusion(f32[8,64,8,32]{1,3,2,0:T(8,128)S(1)} %bitcast.78, f32[8,8,64,64]{2,3,1,0:T(8,128)S(1)} %get-tuple-element.10, f32[8,8,64]{2,1,0:T(8,128)S(1)} %fusion.2, f32[8,8,64]{2,1,0:T(8,128)S(1)} %get-tuple-element.9, f32[8,64,64]{1,2,0:T(8,128)S(1)} %copy.44), kind=kOutput, calls=%fused_computation | convolution fusion | flops 101449728 | bytes 2260992 | tf_op jit(solution)/shard_map/vmap(hij,jhd->ihd)/dot_general | solution.py:32
  123.5 2.3 %copy.46 = f32[8,64,256]{2,1,0:T(8,128)} copy(f32[8,64,256]{1,2,0:T(8,128)} %bitcast.79) | data formatting | bytes 1048576 | tf_op jit(solution)/shard_map/vmap()/reshape | solution.py:32
  125.8 1.9 %fusion.3 = f32[1,8,64,256]{3,2,1,0:T(8,128)S(1)} fusion(f32[8,64,256]{2,1,0:T(8,128)} %copy.46, f32[8,64,1024]{2,1,0:T(8,128)S(1)} %fusion.4, f32[256,256]{1,0:T(8,128)} %param.19, f32[8,8,8,256]{3,2,1,0:T(8,128)} %all-to-all-done), kind=kOutput, calls=%fused_computation.7 | convolution fusion | flops 403308544 | bytes 2359296 | tf_op jit(solution)/shard_map/vmap()/dot_general | solution.py:36
  127.8 0.3 copy.47
  128.1 19.8 %all_to_all.48 = f32[1,8,64,256]{3,1,0,2:T(8,128)S(1)} all-to-all(f32[1,8,64,256]{3,1,0,2:T(8,128)S(1)} %copy.47), channel_id=1, replica_groups=mesh['seq'=4,'res'=8] {'res'}, dimensions={2} | all-to-all | bytes 1048576 | tf_op jit(solution)/shard_map/all_to_all | solution.py:92
  148.0 1.0 copy.48
  (19 shorter events, 0.1 us)
Async XLA Ops:
  0.6 101.9 %copy-start = (f32[256,1024]{1,0:T(8,128)S(1)}, f32[256,1024]{1,0:T(8,128)}, u32[]{:S(2)}) copy-start(f32[256,1024]{1,0:T(8,128)} %param.18) | copy-start | bytes 3145732
  35.0 22.6 %all-to-all-start.1 = ((f32[4,1,32768]{2,1,0:T(1,128)}), f32[4,1,32768]{2,1,0:T(1,128)S(1)}, u32[]{:S(2)}, u32[]{:S(2)}) async-start(f32[4,1,32768]{2,1,0:T(1,128)} %reshape.99), calls=%async_computation.1 | async-start | bytes 1048576 | tf_op jit(solution)/shard_map/all_to_all | solution.py:64
  57.6 42.2 %all-to-all-start = ((f32[8,8,8,256]{3,2,1,0:T(8,128)}), f32[8,8,8,256]{3,2,1,0:T(8,128)}, u32[]{:S(2)}, u32[]{:S(2)}) async-start(f32[8,8,8,256]{3,2,1,0:T(8,128)} %bitcast), calls=%async_computation | async-start | bytes 1048576 | tf_op jit(solution)/shard_map/all_to_all | solution.py:85
  71.9 1.8 %copy-start.3 = (f32[16,8,128]{2,1,0:T(8,128)S(1)}, f32[16,8,128]{2,1,0:T(8,128)}, u32[]{:S(2)}) copy-start(f32[16,8,128]{2,1,0:T(8,128)} %param.11) | copy-start | bytes 196612
  71.9 3.9 %copy-start.5 = (f32[128,8]{0,1:T(8,128)S(1)}, f32[128,8]{0,1:T(8,128)}, u32[]{:S(2)}) copy-start(f32[128,8]{0,1:T(8,128)} %param.16) | copy-start | bytes 12292
  71.9 3.9 %copy-start.6 = (f32[128]{0:T(128)S(1)}, f32[128]{0:T(128)}, u32[]{:S(2)}) copy-start(f32[128]{0:T(128)} %param.15) | copy-start | bytes 1540
  75.6 29.8 %copy-start.2 = (f32[16,8,128]{2,1,0:T(8,128)}, f32[16,8,128]{2,1,0:T(8,128)S(1)}, u32[]{:S(2)}) copy-start(f32[16,8,128]{2,1,0:T(8,128)S(1)} %get-tuple-element.8) | copy-start | bytes 196612
  75.6 26.9 %copy-start.4 = (f32[256]{0:T(256)S(1)}, f32[256]{0:T(256)}, u32[]{:S(2)}) copy-start(f32[256]{0:T(256)} %param.17) | copy-start | bytes 3076
  118.9 1.2 copy-start.1
where the time goes:
time: 150 us; the launch traced here: 149 us
  blocking collectives  86.8 us (58%)
  local copies, waits for them, and re-layouts  23.6 us (16%)
  matrix products  20.3 us (14%)
  other arithmetic  9.14 us (6%)
  starting transfers between devices  8.05 us (5%)
    all_gather x1, blocking collectives, on_device(): left_all = lax.all_gather(left_maps, 'res', axis=2, tiled=True)  25.1 us
    all_to_all x1, blocking collectives, on_device(): lax.all_to_all(attended, 'res', split_axis=2, concat_axis=0, tiled=True)  19.8 us
    all_gather x1, blocking collectives, on_device(): lax.all_gather(right_maps, 'seq', axis=0, tiled=True)  18.5 us
    all_gather x1, blocking collectives, on_device(): bias_rows = lax.all_gather(bias_tile, 'res', axis=2, tiled=True)  14.9 us
    all_gather x1, blocking collectives, on_device(): bias_all = lax.all_gather(bias_rows, 'seq', axis=1, tiled=True)  8.4 us
    dot_general x1, matrix products, row_attention(): jnp.einsum('ihd,jhd->hij', query_map, key_map, precision=precise) + bias_all  5.09 us
    all_to_all x1, starting transfers between devices, on_device(): lax.all_to_all(sequence_grouped_rows, 'res', split_axis=0, concat_axis=2,...  4.34 us
    div x2, local copies, waits for them, and re-layouts, on_device(): summed / seq_total  4 us
  transfers between devices with their start and end apart: 2, of which 0 were waited for; matrix products, arithmetic and copies ran while one was open for 10% of the time, Pallas kernels for 0%

commit v1 on v0

--- a/solution.py
+++ b/solution.py
@@ -62,12 +62,38 @@
     right_maps = both_maps[:, channels:]
     left_all = lax.all_gather(left_maps, "res", axis=2, tiled=True)
     left_rows = lax.all_to_all(left_all, "seq", split_axis=2, concat_axis=0, tiled=True)
-    product = jnp.einsum(
+    count, index, span = (lax.axis_size("seq"), lax.axis_index("seq"), right_maps.shape[0])
+    right = [(i, (i + 1) % count) for i in range(count)]
+    left = [(i, (i - 1) % count) for i in range(count)]
+    half = count // 2
+    from_left = from_right = right_maps
+    total = jnp.einsum(
         "sxi,syj->ijxy",
-        left_rows,
-        lax.all_gather(right_maps, "seq", axis=0, tiled=True),
+        lax.dynamic_slice_in_dim(left_rows, index * span, right_maps.shape[0], axis=0),
+        right_maps,
         precision=precise,
     )
+    for hop in range(1, half + 1):
+        from_left = lax.ppermute(from_left, "seq", right)
+        if hop < count - half:
+            from_right = lax.ppermute(from_right, "seq", left)
+            total = total + jnp.einsum(
+                "sxi,syj->ijxy",
+                lax.dynamic_slice_in_dim(
+                    left_rows, (index + hop) % count * span, from_right.shape[0], axis=0
+                ),
+                from_right,
+                precision=precise,
+            )
+        total = total + jnp.einsum(
+            "sxi,syj->ijxy",
+            lax.dynamic_slice_in_dim(
+                left_rows, (index - hop) % count * span, from_left.shape[0], axis=0
+            ),
+            from_left,
+            precision=precise,
+        )
+    product = total
     summed = product.reshape(row_block, residue_local_count, channels * channels)
     pair_update = jnp.einsum("ijk,kc->ijc", summed / seq_total, w_outer_out, precision=precise)
     updated_pair_array = pair_features + pair_update

time: 150 us -> 163 us (1.087)
  blocking collectives: 86.8 us -> 69.6 us
  matrix products: 20.3 us -> 33.5 us
  waiting for transfers between devices: 0.01 us -> 13.1 us
  starting transfers between devices: 8.05 us -> 11 us
    all_gather x1 -> x0, blocking collectives: 18.5 us -> none  [on_device(): lax.all_gather(right_maps, 'seq', axis=0, tiled=True)]
    dot_general x1 -> x4, matrix products: 3.15 us -> 17.5 us  [the longest x2 9.31 us: on_device(): jnp.einsum('sxi,syj->ijxy', lax.dynamic_slice_in_dim(left_rows, (index -...]
    ppermute x0 -> x3, waiting for transfers between devices: none -> 13.1 us  [the longest x2 13.1 us: on_device(): from_left = lax.ppermute(from_left, 'seq', right)]
    ppermute x0 -> x3, starting transfers between devices: none -> 2.95 us  [the longest x2 2.03 us: on_device(): from_left = lax.ppermute(from_left, 'seq', right)]
    unnamed x16 -> x20, local copies, waits for them, and re-layouts: 3.91 us -> 3.91 us
  transfers between devices with their start and end apart: 2 -> 5, of which waited for: 0 -> 1; matrix products, arithmetic and copies ran while one was open for 10% -> 17% of each run, Pallas kernels for 0% -> 0%
where the time goes in v1:
time: 163 us; the launch traced here: 162 us
  blocking collectives  69.6 us (43%)
  matrix products  33.5 us (21%)
  local copies, waits for them, and re-layouts  24.4 us (15%)
  waiting for transfers between devices  13.1 us (8%)
  starting transfers between devices  11 us (7%)
  other arithmetic  9.14 us (6%)
    all_gather x1, blocking collectives, on_device(): left_all = lax.all_gather(left_maps, 'res', axis=2, tiled=True)  25.1 us
    all_to_all x1, blocking collectives, on_device(): lax.all_to_all(attended, 'res', split_axis=2, concat_axis=0, tiled=True)  19.8 us
    all_gather x1, blocking collectives, on_device(): bias_rows = lax.all_gather(bias_tile, 'res', axis=2, tiled=True)  14.9 us
    ppermute x2, waiting for transfers between devices, on_device(): from_left = lax.ppermute(from_left, 'seq', right)  13.1 us
    all_gather x1, blocking collectives, on_device(): bias_all = lax.all_gather(bias_rows, 'seq', axis=1, tiled=True)  9.75 us
    dot_general x2, matrix products, on_device(): jnp.einsum('sxi,syj->ijxy', lax.dynamic_slice_in_dim(left_rows, (index -...  9.31 us
    dot_general x1, matrix products, row_attention(): jnp.einsum('ihd,jhd->hij', query_map, key_map, precision=precise) + bias_all  5.09 us
    dot_general x1, matrix products, on_device(): jnp.einsum('sxi,syj->ijxy', lax.dynamic_slice_in_dim(left_rows, (index +...  4.47 us
  transfers between devices with their start and end apart: 5, of which 1 were waited for; matrix products, arithmetic and copies ran while one was open for 17% of the time, Pallas kernels for 0%

profile of v1, /device:TPU:0, one launch (start us, length us, event | category | flops | bytes accessed | tf_op | source)
XLA Modules:
  0.0 161.7 jit_solution(4749588379017308565)
XLA Ops:
  0.6 1.3 reduce_sum.65
  1.9 1.3 multiply_reduce_fusion
  3.2 1.7 %convolution_bitcast_fusion = f32[64,64,8]{1,2,0:T(8,128)S(1)} fusion(f32[64,8,256]{2,1,0:T(8,128)} %param.10, f32[256]{0:T(256)} %param.12, f32[64,8]{1,0:T(8,128)S(1)} %add_rsqrt_fusion, f32[64,8]{1,0:T(8,128)S(1)} %broadcast_multiply_fusion, f32[256,64]{0,1:T(8,128)} %param.13), kind=kOutput, calls=%fused_computation.8 | convolution fusion | flops 101056512 | bytes 726016 | tf_op jit(solution)/shard_map/src,cd->sdr/dot_general | solution.py:60
  4.9 0.9 slice_bitcast_fusion
  5.8 25.1 %all_gather.9 = f32[64,32,64]{1,2,0:T(8,128)S(1)} all-gather(f32[64,32,8]{1,2,0:T(8,128)S(1)} %get-tuple-element.6), channel_id=1, replica_groups=mesh['seq'=4,'res'=8] {'res'}, dimensions={2}, use_global_device_ids=true | all-gather | bytes 589824 | tf_op jit(solution)/shard_map/all_gather | solution.py:63
  30.9 2.1 %copy.45 = f32[64,32,64]{0,1,2:T(8,128)} copy(f32[64,32,64]{1,2,0:T(8,128)S(1)} %all_gather.9) | data formatting | bytes 1048576 | tf_op jit(solution)/shard_map/all_gather | solution.py:63
  33.0 2.7 %reshape.104 = f32[4,1,32768]{2,1,0:T(1,128)} reshape(f32[64,32,64]{2,1,0:T(8,128)} %bitcast.87) | data formatting | bytes 1048576
  35.7 3.7 %all-to-all-start.1 = ((f32[4,1,32768]{2,1,0:T(1,128)}), f32[4,1,32768]{2,1,0:T(1,128)S(1)}, u32[]{:S(2)}, u32[]{:S(2)}) async-start(f32[4,1,32768]{2,1,0:T(1,128)} %reshape.104), calls=%async_computation.1 | async-start | bytes 1048576 | tf_op jit(solution)/shard_map/all_to_all | solution.py:64
  39.4 2.0 %collective-permute-start.1 = (f32[64,32,8]{1,2,0:T(8,128)}, f32[64,32,8]{1,2,0:T(8,128)}, u32[]{:S(2)}, u32[]{:S(2)}) collective-permute-start(f32[64,32,8]{1,2,0:T(8,128)} %get-tuple-element.7), channel_id=1, source_target_pairs={{0,8},{8,16},{16,24},{24,0},{1,9},{9,17},{17,25},{25,1},{2,10},{10... | collective-permute-start | bytes 196616 | tf_op jit(solution)/shard_map/ppermute | solution.py:77
  41.4 0.9 collective-permute-start
  42.4 13.1 %collective-permute-done.1 = f32[64,32,8]{1,2,0:T(8,128)} collective-permute-done((f32[64,32,8]{1,2,0:T(8,128)}, f32[64,32,8]{1,2,0:T(8,128)}, u32[]{:S(2)}, u32[]{:S(2)}) %collective-permute-start.1) | collective-permute-done | bytes 65568 | tf_op jit(solution)/shard_map/ppermute | solution.py:77
  55.5 4.3 %all-to-all-start = ((f32[8,8,8,256]{3,2,1,0:T(8,128)}), f32[8,8,8,256]{3,2,1,0:T(8,128)}, u32[]{:S(2)}, u32[]{:S(2)}) async-start(f32[8,8,8,256]{3,2,1,0:T(8,128)} %bitcast), calls=%async_computation | async-start | bytes 1048576 | tf_op jit(solution)/shard_map/all_to_all | solution.py:111
  59.8 0.5 broadcast.100
  60.3 2.1 %reduce.2 = f32[4,32768]{1,0:T(4,128)S(1)} reduce(f32[4,1,32768]{2,1,0:T(1,128)S(1)} %all-to-all-done.1, f32[]{:T(128)} %broadcast.100), dimensions={1}, to_apply=%all_to_all.38.reduce_sub_computation | reduce | bytes 1048580 | tf_op jit(solution)/shard_map/all_to_all | solution.py:64
  62.5 0.5 reshape.105
  63.0 0.7 copy.85
  63.7 0.6 all_to_all.41
  64.3 4.7 %fusion.25 = f32[32,8,32,16]{2,0,3,1:T(8,128)S(1)} fusion(f32[64,32,8,1]{1,2,0,3:T(8,128)} %bitcast.17, f32[256,32,16]{0,1,2:T(8,128)S(1)} %all_to_all.41, s32[]{:T(128)S(6)} %select_n.31), kind=kOutput, calls=%fused_computation.36 | convolution fusion | flops 100663296 | bytes 851972 | tf_op jit(solution)/shard_map/sxi,syj->ijxy/dot_general | solution.py:88
  69.0 4.5 %fusion.28 = f32[32,8,32,16]{2,0,3,1:T(8,128)S(1)} fusion(f32[64,32,8,1]{1,2,0,3:T(8,128)} %bitcast.15, f32[256,32,16]{0,1,2:T(8,128)S(1)} %all_to_all.41, s32[]{:T(128)S(6)} %select_n.29), kind=kOutput, calls=%fused_computation.39 | convolution fusion | flops 100663296 | bytes 851972 | tf_op jit(solution)/shard_map/sxi,syj->ijxy/dot_general | solution.py:80
  73.5 3.7 %fusion.31 = f32[32,8,32,16]{2,0,3,1:T(8,128)S(1)} fusion(f32[64,32,8,1]{1,2,0,3:T(8,128)S(1)} %get-tuple-element.5, f32[256,32,16]{0,1,2:T(8,128)S(1)} %all_to_all.41, s32[]{:T(128)S(6)} %select_n.27), kind=kOutput, calls=%fused_computation.42 | convolution fusion | flops 100663296 | bytes 1048580 | tf_op jit(solution)/shard_map/sxi,syj->ijxy/dot_general | solution.py:70
  77.3 4.7 %multiply_bitcast_fusion = f32[16,8,32,32]{2,3,0,1:T(8,128)S(1)} fusion(f32[32,8,32,16]{2,0,3,1:T(8,128)S(1)} %fusion.25, f32[32,8,32,16]{2,0,3,1:T(8,128)S(1)} %fusion.31, f32[32,8,32,16]{2,0,3,1:T(8,128)S(1)} %fusion.28, f32[64,32,8,1]{1,2,0,3:T(8,128)} %bitcast.19, f32[256,32,16]{0,1,2:T(8,128)} %copy-done.1, s32[]{:T(128)S(6)} %select_n.33), kind=kOutput, calls=%fused_computation.3 | convolution fusion | flops 101187584 | bytes 2621444 | tf_op jit(solution)/shard_map/sxi,syj->ijxy/dot_general | solution.py:88
  81.9 1.9 %copy.51 = f32[16,8,32,32]{3,2,1,0:T(8,128)} copy(f32[16,8,32,32]{2,3,0,1:T(8,128)S(1)} %multiply_bitcast_fusion) | data formatting | bytes 1048576 | tf_op jit(solution)/shard_map/div | solution.py:98
  83.8 2.5 %div.50 = f32[16,8,1024]{2,1,0:T(8,128)S(1)} reshape(f32[16,8,32,32]{3,2,1,0:T(8,128)} %copy.51) | data formatting | bytes 1048576 | tf_op jit(solution)/shard_map/div | solution.py:98
  86.3 0.7 fusion.59
  87.1 0.2 multiply_reduce_fusion.2
  87.3 0.3 convolution_bitcast_fusion.1
  87.6 14.9 %all_gather.10 = f32[8,16,64]{0,2,1:T(8,128)S(1)} all-gather(f32[8,16,8]{0,2,1:T(8,128)S(1)} %convolution_bitcast_fusion.1), channel_id=1, replica_groups=mesh['seq'=4,'res'=8] {'res'}, dimensions={2}, use_global_device_ids=true | all-gather | bytes 36864 | tf_op jit(solution)/shard_map/all_gather | solution.py:103
  102.5 0.2 copy.52
  102.7 9.8 %all_gather.11 = f32[8,64,64]{2,0,1:T(8,128)S(1)} all-gather(f32[8,16,64]{2,0,1:T(8,128)S(1)} %copy.52), channel_id=1, replica_groups=mesh['seq'=4,'res'=8] {'seq'}, dimensions={1}, use_global_device_ids=true | all-gather | bytes 163840 | tf_op jit(solution)/shard_map/all_gather | solution.py:104
  112.4 0.1 copy.53
  112.6 1.2 bitcast_reduce_fusion
  113.8 1.3 multiply_reduce_fusion.1
  115.2 0.1 rsqrt.28
  115.2 0.1 div.42
  115.3 2.9 %fusion.4 = f32[8,64,1024]{2,1,0:T(8,128)S(1)} fusion(f32[256,1024]{1,0:T(8,128)S(1)} %copy-done, f32[256]{0:T(256)S(1)} %copy-done.6, f32[8,64]{1,0:T(8,128)S(1)} %rsqrt.28, f32[8,64]{1,0:T(8,128)S(1)} %div.42, f32[8,8,8,256]{3,2,1,0:T(8,128)} %all-to-all-done), kind=kOutput, calls=%fused_computation.11 | convolution fusion | flops 1611005952 | bytes 3675136 | tf_op jit(solution)/shard_map/vmap()/dot_general | solution.py:21
  118.3 1.2 fusion.58
  119.5 2.4 %copy.43 = f32[8,64,256]{1,2,0:T(8,128)} copy(f32[8,64,256]{2,1,0:T(8,128)} %get-tuple-element.3) | data formatting | bytes 1048576 | tf_op jit(solution)/shard_map/vmap()/mul | solution.py:24
  121.9 2.4 %copy.44 = f32[8,64,256]{1,2,0:T(8,128)} copy(f32[8,64,256]{2,1,0:T(8,128)} %get-tuple-element.2) | data formatting | bytes 1048576 | tf_op jit(solution)/shard_map/vmap()/slice | solution.py:27
  124.2 2.4 %copy.42 = f32[8,64,256]{1,2,0:T(8,128)} copy(f32[8,64,256]{2,1,0:T(8,128)} %get-tuple-element.4) | data formatting | bytes 1048576 | tf_op jit(solution)/shard_map/vmap()/slice | solution.py:28
  126.6 5.1 %add_reduce_fusion = (f32[8,8,64]{2,1,0:T(8,128)S(1)}, f32[8,8,64,64]{2,3,1,0:T(8,128)S(1)}) fusion(f32[8,64,64]{1,2,0:T(8,128)S(1)} %copy.53, f32[8,64,8,32]{1,3,2,0:T(8,128)} %bitcast.85, f32[8,64,8,32]{1,3,2,0:T(8,128)} %bitcast.86), kind=kOutput, calls=%fused_computation.4 | convolution fusion | flops 101183488 | bytes 2244608 | tf_op jit(solution)/shard_map/vmap(ihd,jhd->hij)/dot_general | solution.py:30
  131.8 0.5 fusion.2
  132.3 0.7 copy-done.2
  133.0 3.3 %fusion = f32[8,8,32,64]{3,2,1,0:T(8,128)} fusion(f32[8,64,8,32]{1,3,2,0:T(8,128)S(1)} %bitcast.91, f32[8,8,64,64]{2,3,1,0:T(8,128)S(1)} %get-tuple-element.11, f32[8,8,64]{2,1,0:T(8,128)S(1)} %fusion.2, f32[8,8,64]{2,1,0:T(8,128)S(1)} %get-tuple-element.10, f32[8,64,64]{1,2,0:T(8,128)S(1)} %copy.53), kind=kOutput, calls=%fused_computation | convolution fusion | flops 101449728 | bytes 2260992 | tf_op jit(solution)/shard_map/vmap(hij,jhd->ihd)/dot_general | solution.py:32
  136.3 2.3 %copy.55 = f32[8,64,256]{2,1,0:T(8,128)} copy(f32[8,64,256]{1,2,0:T(8,128)} %bitcast.92) | data formatting | bytes 1048576 | tf_op jit(solution)/shard_map/vmap()/reshape | solution.py:32
  138.6 1.9 %fusion.3 = f32[1,8,64,256]{3,2,1,0:T(8,128)S(1)} fusion(f32[8,64,256]{2,1,0:T(8,128)} %copy.55, f32[8,64,1024]{2,1,0:T(8,128)S(1)} %fusion.4, f32[256,256]{1,0:T(8,128)} %param.19, f32[8,8,8,256]{3,2,1,0:T(8,128)} %all-to-all-done), kind=kOutput, calls=%fused_computation.7 | convolution fusion | flops 403308544 | bytes 2359296 | tf_op jit(solution)/shard_map/vmap()/dot_general | solution.py:36
  140.6 0.3 copy.56
  140.9 19.8 %all_to_all.48 = f32[1,8,64,256]{3,1,0,2:T(8,128)S(1)} all-to-all(f32[1,8,64,256]{3,1,0,2:T(8,128)S(1)} %copy.56), channel_id=1, replica_groups=mesh['seq'=4,'res'=8] {'res'}, dimensions={2} | all-to-all | bytes 1048576 | tf_op jit(solution)/shard_map/all_to_all | solution.py:118
  160.8 1.0 copy.57
  (30 shorter events, 0.1 us)
Async XLA Ops:
  0.6 114.7 %copy-start = (f32[256,1024]{1,0:T(8,128)S(1)}, f32[256,1024]{1,0:T(8,128)}, u32[]{:S(2)}) copy-start(f32[256,1024]{1,0:T(8,128)} %param.18) | copy-start | bytes 3145732
  35.7 19.8 %all-to-all-start.1 = ((f32[4,1,32768]{2,1,0:T(1,128)}), f32[4,1,32768]{2,1,0:T(1,128)S(1)}, u32[]{:S(2)}, u32[]{:S(2)}) async-start(f32[4,1,32768]{2,1,0:T(1,128)} %reshape.104), calls=%async_computation.1 | async-start | bytes 1048576 | tf_op jit(solution)/shard_map/all_to_all | solution.py:64
  39.4 16.1 %collective-permute-start.1 = (f32[64,32,8]{1,2,0:T(8,128)}, f32[64,32,8]{1,2,0:T(8,128)}, u32[]{:S(2)}, u32[]{:S(2)}) collective-permute-start(f32[64,32,8]{1,2,0:T(8,128)} %get-tuple-element.7), channel_id=1, source_target_pairs={{0,8},{8,16},{16,24},{24,0},{1,9},{9,17},{17,25},{25,1},{2,10},{10... | collective-permute-start | bytes 196616 | tf_op jit(solution)/shard_map/ppermute | solution.py:77
  41.4 27.6 %collective-permute-start = (f32[64,32,8]{1,2,0:T(8,128)}, f32[64,32,8]{1,2,0:T(8,128)}, u32[]{:S(2)}, u32[]{:S(2)}) collective-permute-start(f32[64,32,8]{1,2,0:T(8,128)} %get-tuple-element.7), channel_id=1, source_target_pairs={{0,24},{8,0},{16,8},{24,16},{1,25},{9,1},{17,9},{25,17},{2,26},{10... | collective-permute-start | bytes 196616 | tf_op jit(solution)/shard_map/ppermute | solution.py:79
  55.5 21.8 %collective-permute-start.2 = (f32[64,32,8]{1,2,0:T(8,128)}, f32[64,32,8]{1,2,0:T(8,128)}, u32[]{:S(2)}, u32[]{:S(2)}) collective-permute-start(f32[64,32,8]{1,2,0:T(8,128)} %collective-permute-done.1), channel_id=1, source_target_pairs={{0,8},{8,16},{16,24},{24,0},{1,9},{9,17},{17,25},{25,1},{2,10},{10... | collective-permute-start | bytes 196616 | tf_op jit(solution)/shard_map/ppermute | solution.py:77
  55.5 57.1 %all-to-all-start = ((f32[8,8,8,256]{3,2,1,0:T(8,128)}), f32[8,8,8,256]{3,2,1,0:T(8,128)}, u32[]{:S(2)}, u32[]{:S(2)}) async-start(f32[8,8,8,256]{3,2,1,0:T(8,128)} %bitcast), calls=%async_computation | async-start | bytes 1048576 | tf_op jit(solution)/shard_map/all_to_all | solution.py:111
  64.3 9.2 %copy-start.1 = (f32[256,32,16]{0,1,2:T(8,128)}, f32[256,32,16]{0,1,2:T(8,128)S(1)}, u32[]{:S(2)}) copy-start(f32[256,32,16]{0,1,2:T(8,128)S(1)} %all_to_all.41) | copy-start | bytes 1572868
  83.8 2.5 %copy-start.3 = (f32[1024,128]{1,0:T(8,128)S(1)}, f32[1024,128]{1,0:T(8,128)}, u32[]{:S(2)}) copy-start(f32[1024,128]{1,0:T(8,128)} %param.14) | copy-start | bytes 1572868
  83.8 2.5 %copy-start.5 = (f32[16,8,128]{2,1,0:T(8,128)S(1)}, f32[16,8,128]{2,1,0:T(8,128)}, u32[]{:S(2)}) copy-start(f32[16,8,128]{2,1,0:T(8,128)} %param.11) | copy-start | bytes 196612
  83.8 3.5 %copy-start.7 = (f32[128,8]{0,1:T(8,128)S(1)}, f32[128,8]{0,1:T(8,128)}, u32[]{:S(2)}) copy-start(f32[128,8]{0,1:T(8,128)} %param.16) | copy-start | bytes 12292
  83.8 3.5 %copy-start.8 = (f32[128]{0:T(128)S(1)}, f32[128]{0:T(128)}, u32[]{:S(2)}) copy-start(f32[128]{0:T(128)} %param.15) | copy-start | bytes 1540
  87.1 31.2 %copy-start.4 = (f32[16,8,128]{2,1,0:T(8,128)}, f32[16,8,128]{2,1,0:T(8,128)S(1)}, u32[]{:S(2)}) copy-start(f32[16,8,128]{2,1,0:T(8,128)S(1)} %get-tuple-element.9) | copy-start | bytes 196612
  87.1 28.3 %copy-start.6 = (f32[256]{0:T(256)S(1)}, f32[256]{0:T(256)}, u32[]{:S(2)}) copy-start(f32[256]{0:T(256)} %param.17) | copy-start | bytes 3076
  131.7 1.2 copy-start.2
